TPU v7x, 32 devices: a whole 2x2x4 slice. The times are simulated.
32 devices in a mesh: row: 4 (over y, x), col: 8 (over z, core).
Axes of the slice: x: 2, y: 2, z: 4, core: 2. Of those that a mesh axis runs over, the one named last changes fastest.
Arguments:
- tokens: bfloat16 [512, 16384], P('col', 'row'), may hold values from -6 to 6
- weight: bfloat16 [16384, 32768], P('row', 'col'), may hold values from -0.21875 to 0.21875
- logits: float32 [3, 32768], P(None, 'col'), may hold values from -6 to 303
- cotangent: bfloat16 [512, 32768], P('row', 'col'), may hold values from -6 to 6
Outputs:
- mixed_out: bfloat16 [512, 32768], P('row', 'col')
- input_grad: bfloat16 [512, 16384], P('col', 'row')
- weight_grad: bfloat16 [16384, 32768], P('row', 'col')
- logit_grad: float32 [3, 32768], P(None, 'col')
All inputs are finite; a program needn't handle non-finite values.
Results may differ from a plain program's by a relative error of at most 0.0049.
Values may be sent and summed in bfloat16 or wider, within the bound.
No kernel may reach another device: no remote copies, remote signals or barrier semaphores. Data moves between devices by JAX's collectives and lax.ppermute only.
A program may use at most 192 MiB of HBM per device.

v0:
```python
import functools
import math

import jax
import jax.numpy as jnp
from jax import lax
from jax.experimental import pallas as pl
from jax.experimental.pallas import tpu as pltpu
from jax.sharding import PartitionSpec as P


EPSILON = 1e-06
TWO_PI = 2.0 * math.pi
LEVELS = (1.0, 7.0, 127.0)
S0, S1, S2, S3 = 6.28312416, -10.3332539, 5.07633545, -1.09334416
FOLD = S3 * S3


def main_kernel(meta, *refs, nrow, ncol, nd, nj, bd, bj, strip, d0, t0, j0, carry_out, last_out, carry_in):
    nz = ncol // 2
    it = iter(refs)
    take = lambda n: [next(it) for _ in range(n)]
    tok_in, cot_in = take(ncol), take(nrow)
    w_ref, const_ref = take(2)
    take(1 if d0 or j0 else 0)
    out_prev = take(1)[0] if carry_out else None
    in_prev = take(1)[0] if j0 else None
    wg_ref, terms_ref = take(2)
    outs = take(nrow + 1) if last_out else take(1)
    ins = take(1) if carry_in else take(2)
    tok, tokt, cot, out_acc, in_acc, terms, bl_a, bl_b, mg_a, mg_b, sems, sem_out = take(12)
    dn, jn = pl.program_id(0), pl.program_id(1)
    row, col = meta[0], meta[1]
    rows_t, rows_c = tok_in[0].shape[0], cot_in[0].shape[0]
    step = dn * nj + jn
    wide = min(256, bj)

    def prev_copy(tile):
        return pltpu.make_async_copy(
            out_prev.at[j0 // bj + tile], out_acc.at[tile], sem_out.at[tile]
        )

    def out_copy(tile):
        return pltpu.make_async_copy(out_acc.at[tile], outs[0].at[tile], sem_out.at[tile])

    tokens = cot.shape[1]

    def gradient(d, tile, mg):
        def piece(cols):
            mg[:, cols] = jnp.dot(tokt[d], cot[tile, :, cols], preferred_element_type=jnp.float32)

        return [functools.partial(piece, slice(n, n + wide)) for n in range(0, bj, wide)]

    def products(d, tile, bl):
        def out_piece(cols):
            out_acc[tile, :, cols] += jnp.dot(tok[d], bl[:, cols], preferred_element_type=jnp.float32)

        def in_piece(part):
            in_acc[d, part, :] += lax.dot_general(
                cot[tile, part, :], bl[...], (((1,), (1,)), ((), ())), preferred_element_type=jnp.float32
            )

        half = tokens // 2
        outs = [functools.partial(out_piece, slice(n, n + wide)) for n in range(0, bj, wide)]
        return outs + [functools.partial(in_piece, slice(n, n + half)) for n in range(0, tokens, half)]

    @pl.when(step == 0)
    def _():
        copies = []
        for k in range(nrow):
            off = pl.multiple_of((row ^ k) * rows_c, rows_c)
            for n in range(2 * nj):
                src = cot_in[k].at[:, j0 + n * bj : j0 + (n + 1) * bj]
                dst = cot.at[n, pl.ds(off, rows_c), :]
                copies.append(pltpu.make_async_copy(src, dst, sems.at[len(copies)]))
        for k in range(ncol):
            off = pl.multiple_of((col ^ k) * rows_t, rows_t)
            for n in range(nd):
                src = tok_in[k].at[:, t0 + n * bd : t0 + (n + 1) * bd]
                dst = tok.at[n, pl.ds(off, rows_t), :]
                copies.append(pltpu.make_async_copy(src, dst, sems.at[len(copies)]))
        if in_prev is not None:
            copies.append(pltpu.make_async_copy(in_prev, in_acc, sems.at[len(copies)]))
        for copy in copies:
            copy.start()
        if carry_out:
            for tile in range(2 * nj):
                prev_copy(tile).start()
        else:

            @pl.loop(0, 2 * nj)
            def _(tile):
                out_acc[tile] = jnp.zeros(out_acc.shape[1:], jnp.float32)

        if in_prev is None:

            @pl.loop(0, nd)
            def _(d):
                in_acc[d] = jnp.zeros(in_acc.shape[1:], jnp.float32)

        terms[...] = jnp.zeros_like(terms)
        bl_b[...] = jnp.zeros_like(bl_b)
        for copy in copies:
            copy.wait()

        @pl.loop(0, nd)
        def _(d):
            tokt[d] = tok[d].T

        for piece in gradient(0, 0, mg_a):
            piece()

    if carry_out:

        @pl.when(dn == 0)
        def _():
            prev_copy(2 * jn).wait()
            prev_copy(2 * jn + 1).wait()

    def strips(mg, bl, left, lane, tops):
        here = slice(lane, lane + 128)
        cols = slice(left + lane, left + lane + 128)
        inv0, inv2, k0, k1, k2, h0, h1, h2 = [const_ref[n : n + 1, cols] for n in range(8)]
        sums = [None] * 3
        for top in tops:
            part = slice(top, top + strip)
            w = w_ref[part, cols].astype(jnp.float32)
            g = mg[part, here]
            r = w * inv0
            f = r - jnp.round(r)
            y = f * f
            s = (((S3 * y + S2) * y + S1) * y + S0) * f
            x = s * s
            q = 4.0 - x
            a0 = s * (q * lax.rsqrt(q))
            v = 2.0 - x
            z = v * v
            e = z - 1.0
            o = v * (z - 2.0)
            up, down = o + e, o - e
            pq = up * down
            u = w * inv2
            f2 = u - jnp.round(u)
            y2 = f2 * f2
            s2 = (((y2 + S2 / S3) * y2 + S1 / S3) * y2 + S0 / S3) * f2
            x2 = s2 * s2
            q2 = 4.0 / FOLD - x2
            a2 = s2 * (q2 * lax.rsqrt(q2))
            blend = w - a0 * (k0 + k1 * pq) - k2 * a2
            slope = x * (h0 + h1 * (up * up)) + h2 * x2
            bl[part, here] = blend.astype(jnp.bfloat16)
            wg_ref[part, cols] = (g * slope).astype(jnp.bfloat16)
            m0 = g * a0
            for n, val in enumerate((m0, m0 * pq, g * a2)):
                val = val.reshape(strip // 8, 8, 128).sum(0)
                sums[n] = val if sums[n] is None else sums[n] + val
        return sums

    def arithmetic(mg, bl, tile, left, beside):
        n_blocks = bj // 128
        for n in range(n_blocks):
            share = beside[n * len(beside) // n_blocks : (n + 1) * len(beside) // n_blocks]

            @pl.when(step >= 0)
            def _(n=n, share=share):
                lane = n * 128
                for piece in share:
                    piece()
                sums = strips(mg, bl, left, lane, range(0, bd, strip))
                for m in range(3):
                    terms[tile, m, :, lane : lane + 128] += sums[m]

    before = jnp.maximum(step - 1, 0)
    after = jnp.minimum(step + 1, nd * nj - 1)
    left, right = 2 * jn, 2 * jn + 1
    arithmetic(
        mg_a, bl_a, left, 0, gradient(dn, right, mg_b) + products(before // nj, 2 * (before % nj) + 1, bl_b)
    )
    arithmetic(
        mg_b, bl_b, right, bj, gradient(after // nj, 2 * (after % nj), mg_a) + products(dn, left, bl_a)
    )

    @pl.when(step == nd * nj - 1)
    def _():
        for piece in products(nd - 1, 2 * nj - 1, bl_b):
            piece()
        for tile in range(2 * nj):
            for n in range(3):
                terms_ref[n : n + 1, tile * bj : (tile + 1) * bj] = terms[tile, n].sum(0, keepdims=True)

    if last_out:

        @pl.when(step == nd * nj - 1)
        def _():
            for tile in range(2 * nj):
                cols = slice(tile * bj, (tile + 1) * bj)
                for k in range(nrow):
                    off = pl.multiple_of((row ^ k) * rows_c, rows_c)
                    outs[k][:, cols] = out_acc[tile, pl.ds(off, rows_c), :].astype(jnp.bfloat16)
                total = jnp.zeros((8, bj), jnp.float32)
                for top in range(0, tokens, 32):
                    val = out_acc[tile, top : top + 32, :] * cot[tile, top : top + 32, :].astype(jnp.float32)
                    total = total + val.reshape(4, 8, bj).sum(0)
                outs[nrow][:, cols] = total.sum(0, keepdims=True)

    else:

        @pl.when(dn == nd - 1)
        def _():
            out_copy(left).start()

        @pl.when((dn == nd - 1) & (jn > 0))
        def _():
            out_copy(left - 1).start()

        @pl.when(step == nd * nj - 1)
        def _():
            out_copy(2 * nj - 1).start()
            for tile in range(2 * nj):
                out_copy(tile).wait()

    @pl.when(step == nd * nj - 1)
    def _():
        if carry_in:
            ins[0][...] = in_acc[...]
        else:
            core = col & 1
            for d in range(nd):
                cols = slice(d * bd, (d + 1) * bd)
                for k in range(nz):
                    base = ((col >> 1) ^ k) * 2
                    mine = pl.multiple_of((base + core) * rows_t, rows_t)
                    other = pl.multiple_of((base + 1 - core) * rows_t, rows_t)
                    ins[0][k, :, cols] = in_acc[d, pl.ds(mine, rows_t), :]
                    ins[1][k, :, cols] = in_acc[d, pl.ds(other, rows_t), :].astype(jnp.bfloat16)


def main_call(meta, toks, cots, weight, consts, wg, out_prev, in_prev, *, rows, t0, cols, final, bd=256, bj=512, strip=16):
    nrow, ncol = len(cots), len(toks)
    nz = ncol // 2
    (d0, depth), (j0, width) = rows, cols
    bd, bj = min(bd, depth), min(bj, weight.shape[1] // 4)
    nd, nj = depth // bd, width // (2 * bj)
    rows_t, rows_c = toks[0].shape[0], cots[0].shape[0]
    tokens = rows_t * ncol
    carry_in = j0 + width < weight.shape[1]
    bf, f32 = jnp.bfloat16, jnp.float32
    hbm = pl.BlockSpec(memory_space=pl.ANY)
    tile_at = lambda d, j, m: (d0 // bd + d, j0 // (2 * bj) + j)
    shape = jax.ShapeDtypeStruct

    def whole(dims, kind):
        return pl.BlockSpec(dims, lambda d, j, m, n=len(dims): (0,) * n), shape(dims, kind)

    extra = [x for x in (wg, out_prev, in_prev) if x is not None]
    outs = [
        (pl.BlockSpec((bd, 2 * bj), tile_at), shape(weight.shape, bf)),
        whole((3, width), f32),
    ]
    if final:
        outs += [whole((rows_c, width), bf)] * nrow + [whole((1, width), f32)]
    else:
        outs += [(hbm, shape((2 * nj, tokens, bj), f32))]
    if carry_in:
        outs += [whole((nd, tokens, bd), f32)]
    else:
        outs += [whole((nz, rows_t, depth), f32), whole((nz, rows_t, depth), bf)]
    n_in = 1 + ncol + nrow + 2
    grid_spec = pltpu.PrefetchScalarGridSpec(
        num_scalar_prefetch=1,
        grid=(nd, nj),
        in_specs=[hbm] * (nrow + ncol)
        + [
            pl.BlockSpec((bd, 2 * bj), tile_at),
            pl.BlockSpec((8, 2 * bj), lambda d, j, m: (0, j0 // (2 * bj) + j)),
        ]
        + [hbm] * len(extra),
        out_specs=[spec for spec, _ in outs],
        scratch_shapes=[
            pltpu.VMEM((nd, tokens, bd), bf),
            pltpu.VMEM((nd, bd, tokens), bf),
            pltpu.VMEM((2 * nj, tokens, bj), bf),
            pltpu.VMEM((2 * nj, tokens, bj), f32),
            pltpu.VMEM((nd, tokens, bd), f32),
            pltpu.VMEM((2 * nj, 3, 8, bj), f32),
            pltpu.VMEM((bd, bj), bf),
            pltpu.VMEM((bd, bj), bf),
            pltpu.VMEM((bd, bj), f32),
            pltpu.VMEM((bd, bj), f32),
            pltpu.SemaphoreType.DMA((2 * nj * nrow + nd * ncol + 1,)),
            pltpu.SemaphoreType.DMA((2 * nj,)),
        ],
    )
    return pl.pallas_call(
        functools.partial(
            main_kernel, nrow=nrow, ncol=ncol, nd=nd, nj=nj, bd=bd, bj=bj, strip=strip, d0=d0, t0=t0,
            j0=j0, carry_out=out_prev is not None, last_out=final, carry_in=carry_in,
        ),
        grid_spec=grid_spec,
        out_shape=[out for _, out in outs],
        input_output_aliases={} if wg is None else {n_in: 0},
        compiler_params=pltpu.CompilerParams(vmem_limit_bytes=63 * 1024 * 1024),
        cost_estimate=pl.CostEstimate(
            flops=20 * depth * width * tokens,
            bytes_accessed=4 * depth * width,
            transcendentals=2 * depth * width,
        ),
        name="main_kernel",
    )(meta, *toks, *cots, weight, consts, *extra)


def swap(value, axis, size, k):
    return lax.ppermute(value, axis, [(i, i ^ k) for i in range(size)])


def gather_cotangent(nrow, mine):
    if nrow != 4:
        return [mine] + [swap(mine, "row", nrow, k) for k in range(1, nrow)]
    one, two = [swap(mine, "row", nrow, k) for k in (1, 2)]
    half = mine.shape[0] // 2
    far = [swap(two[:half], "row", nrow, 1), swap(one[half:], "row", nrow, 2)]
    return [mine, one, two, jnp.concatenate(far, axis=0)]


def layer(nrow, ncol, tokens, weight, logits, cotangent):
    nz = ncol // 2
    f32, bf = jnp.float32, jnp.bfloat16
    depth, width = weight.shape
    cut = depth // 4

    def gather_tokens(t):
        toks = []
        for t in [t] + [swap(t, "col", ncol, 2 * k) for k in range(1, nz)]:
            toks += [t, swap(t, "col", ncol, 1)]
        return toks

    first = gather_tokens(tokens[:, :cut])
    cots = gather_cotangent(nrow, cotangent)
    rest = gather_tokens(tokens[:, cut:])
    peak = jnp.max(jnp.abs(weight), axis=0, keepdims=True).astype(f32)
    for other in [swap(peak, "row", nrow, k) for k in range(1, nrow)]:
        peak = jnp.maximum(peak, other)
    shares = jax.nn.softmax(logits, axis=0)
    spacing = [(peak + EPSILON) / level for level in LEVELS]
    scale = [spacing[n] / (2.0 * TWO_PI) * (1.0, 1.0, -FOLD)[n] for n in range(3)]
    consts = jnp.concatenate(
        [1.0 / spacing[0], 1.0 / spacing[2]]
        + [shares[n : n + 1] * scale[n] for n in range(3)]
        + [shares[0:1] * 0.5, shares[1:2] * 0.5, shares[2:3] * (0.5 * FOLD)],
        axis=0,
    )
    meta = jnp.stack([lax.axis_index("row"), lax.axis_index("col")]).astype(jnp.int32)

    calls = [
        (first, (0, cut), 0, (0, width), False),
        (rest, (cut, 2 * cut), 0, (0, width), False),
        (rest, (3 * cut, cut), 2 * cut, (0, width // 2), True),
        (rest, (3 * cut, cut), 2 * cut, (width // 2, width // 2), True),
    ]
    wg = out_prev = in_prev = None
    parts, commons, mixed, inputs = [], [], [], []
    for toks, rows, t0, cols, final in calls:
        wg, part, *res = main_call(
            meta, toks, cots, weight, consts, wg, out_prev, in_prev, rows=rows, t0=t0, cols=cols, final=final
        )
        parts.append(part)
        if final:
            outs, common, res = res[:nrow], res[nrow], res[nrow + 1 :]
            commons.append(common)
            far = [swap(outs[k], "row", nrow, k) for k in range(1, nrow)]
            mixed.append(sum([outs[0].astype(f32)] + [x.astype(f32) for x in far]).astype(bf))
        else:
            out_prev, res = res[0], res[1:]
        if cols[0] + cols[1] < width:
            in_prev = res[0]
        else:
            keep, send = res
            got = swap(send, "col", ncol, 1)
            sums = [keep[k] + got[k].astype(f32) for k in range(nz)]
            far = [swap(sums[k].astype(bf), "col", ncol, 2 * k) for k in range(1, nz)]
            inputs.append(sum([sums[0]] + [x.astype(f32) for x in far]).astype(bf))
    mixed_out = jnp.concatenate(mixed, axis=1)
    input_grad = jnp.concatenate(inputs, axis=1)

    parts = parts[0] + parts[1] + jnp.concatenate(parts[2:], axis=1)
    sines = jnp.concatenate([scale[n] * parts[n : n + 1] for n in range(3)], axis=0)
    common = jnp.concatenate(commons, axis=1) + jnp.sum(shares * sines, axis=0, keepdims=True)
    terms = common - sines
    terms = sum([terms] + [swap(terms, "row", nrow, k) for k in range(1, nrow)])
    logit_grad = shares * (terms - jnp.sum(shares * terms, axis=0, keepdims=True))
    return mixed_out, input_grad, wg, logit_grad


def solution(mesh):
    in_specs = (P("col", "row"), P("row", "col"), P(None, "col"), P("row", "col"))
    out_specs = (P("row", "col"), P("col", "row"), P("row", "col"), P(None, "col"))
    nrow, ncol = mesh.shape["row"], mesh.shape["col"]
    body = functools.partial(layer, nrow, ncol)
    return jax.shard_map(body, mesh=mesh, in_specs=in_specs, out_specs=out_specs, check_vma=False)
```

profile of v0, /device:TPU:0, one launch (start us, length us, event | category | flops | bytes accessed | tf_op | source)
XLA Modules:
  0.0 410.6 jit_solution(13389650597320505308)
XLA Ops:
  0.7 11.4 %abs_reduce_fusion = bf16[4096]{0:T(1024)(128)(2,1)S(1)} fusion(bf16[4096,4096]{1,0:T(8,128)(2,1)} %refs_12_.7), kind=kLoop, calls=%fused_computation | loop fusion | flops 33550336 | bytes 33562624 | tf_op jit(solution)/shard_map/reduce_max | solution.py:340
  12.1 4.0 collective-permute-start.13
  16.7 1.9 collective-permute-start.8
  18.6 1.5 collective-permute-start.7
  21.5 1.6 slice.111.refs_0_
  23.1 1.0 slice.105.refs_0_
  24.1 3.7 collective-permute-start.19
  28.6 1.7 slice_multiply_fusion.3
  30.3 11.0 %collective-permute-done.8.refs_10_ = bf16[128,4096]{1,0:T(8,128)(2,1)S(1)} collective-permute-done((bf16[128,4096]{1,0:T(8,128)(2,1)S(1)}, bf16[128,4096]{1,0:T(8,128)(2,1)S(1)}, u32[]{:S(2)}, u32[]{:S(2)}) %collective-permute-start.8) | collective-permute-done | bytes 1048608 | tf_op jit(solution)/shard_map/ppermute | solution.py:313
  43.0 1.6 collective-permute-start.9
  45.6 1.4 collective-permute-start.10
  48.1 1.6 concatenate.31.refs_13_
  49.7 6.1 %collective-permute-done.9 = bf16[64,4096]{1,0:T(8,128)(2,1)} collective-permute-done((bf16[64,4096]{1,0:T(8,128)(2,1)}, bf16[64,4096]{1,0:T(8,128)(2,1)}, u32[]{:S(2)}, u32[]{:S(2)}) %collective-permute-start.9) | collective-permute-done | bytes 524320 | tf_op jit(solution)/shard_map/ppermute | solution.py:313
  55.8 1.9 constant_dynamic-update-slice_fusion.1
  57.7 3.4 collective-permute-start.5
  63.8 7.8 %collective-permute-done.5.refs_6_ = bf16[64,3072]{1,0:T(8,128)(2,1)S(1)} collective-permute-done((bf16[64,3072]{1,0:T(8,128)(2,1)S(1)}, bf16[64,3072]{1,0:T(8,128)(2,1)S(1)}, u32[]{:S(2)}, u32[]{:S(2)}) %collective-permute-start.5) | collective-permute-done | bytes 393248 | tf_op jit(solution)/shard_map/ppermute | solution.py:313
  71.6 23.8 %collective-permute-done.3.refs_4_ = bf16[64,3072]{1,0:T(8,128)(2,1)} collective-permute-done((bf16[64,3072]{1,0:T(8,128)(2,1)S(1)}, bf16[64,3072]{1,0:T(8,128)(2,1)}, u32[]{:S(2)}, u32[]{:S(2)}) %collective-permute-start.3) | collective-permute-done | bytes 393248 | tf_op jit(solution)/shard_map/ppermute | solution.py:313
  96.0 53.5 %main_kernel.4 = (bf16[4096,4096]{1,0:T(8,128)(2,1)}, f32[3,4096]{1,0:T(4,128)}, f32[8,512,512]{2,1,0:T(8,128)}, f32[4,64,1024]{2,1,0:T(8,128)}, bf16[4,64,1024]{2,1,0:T(8,128)(2,1)}) custom-call(s32[2]{0:T(128)} %pad_add_fusion.meta, bf16[64,1024]{1,0:T(8,128)(2,1)} %slice.111.refs_0_, bf16[64,1024]{1,0:T(8,128)(2,1)} %copy-done.20, ...), custom_call_target="tpu_custom_call" | custom-call | flops 42949672960 | bytes 16777216 | tf_op jit(solution)/shard_map/main_kernel/pallas_call | solution.py:294
  149.6 101.9 %main_kernel.5 = (bf16[4096,4096]{1,0:T(8,128)(2,1)}, f32[3,4096]{1,0:T(4,128)}, f32[8,512,512]{2,1,0:T(8,128)}, f32[4,64,2048]{2,1,0:T(8,128)}, bf16[4,64,2048]{2,1,0:T(8,128)(2,1)}) custom-call(s32[2]{0:T(128)} %pad_add_fusion.meta, bf16[64,3072]{1,0:T(8,128)(2,1)} %copy-done.3, ...), custom_call_target="tpu_custom_call", output_to_operand_aliasing={{0}: (15, {})} | custom-call | flops 85899345920 | bytes 33554432 | tf_op jit(solution)/shard_map/main_kernel/pallas_call | solution.py:294
  251.5 31.3 %main_kernel.6 = (bf16[4096,4096]{1,0:T(8,128)(2,1)}, f32[3,2048]{1,0:T(4,128)}, bf16[128,2048]{1,0:T(8,128)(2,1)}, bf16[128,2048]{1,0:T(8,128)(2,1)}, bf16[128,...) custom-call(s32[2]{0:T(128)} %pad_add_fusion.meta, ...), custom_call_target="tpu_custom_call", output_to_operand_aliasing={{0}: (15, {})} | custom-call | flops 21474836480 | bytes 8388608 | tf_op jit(solution)/shard_map/main_kernel/pallas_call | solution.py:294
  282.9 32.0 %main_kernel.7 = (bf16[4096,4096]{1,0:T(8,128)(2,1)}, f32[3,2048]{1,0:T(4,128)}, bf16[128,2048]{1,0:T(8,128)(2,1)}, bf16[128,2048]{1,0:T(8,128)(2,1)}, bf16[128,...) custom-call(s32[2]{0:T(128)} %pad_add_fusion.meta, ...), custom_call_target="tpu_custom_call", output_to_operand_aliasing={{0}: (15, {})} | custom-call | flops 21474836480 | bytes 8388608 | tf_op jit(solution)/shard_map/main_kernel/pallas_call | solution.py:294
  316.9 1.4 collective-permute-start.40
  318.3 1.6 collective-permute-start.41
  320.4 1.4 collective-permute-start.21
  321.9 1.4 collective-permute-start.22
  324.0 1.2 collective-permute-start.23
  325.2 1.0 collective-permute-start.24
  327.1 8.6 %collective-permute-done.21 = bf16[128,2048]{1,0:T(8,128)(2,1)S(1)} collective-permute-done((bf16[128,2048]{1,0:T(8,128)(2,1)}, bf16[128,2048]{1,0:T(8,128)(2,1)S(1)}, u32[]{:S(2)}, u32[]{:S(2)}) %collective-permute-start.21) | collective-permute-done | bytes 524320 | tf_op jit(solution)/shard_map/ppermute | solution.py:313
  335.7 1.1 collective-permute-start.25
  336.8 10.5 %collective-permute-done.22 = bf16[128,2048]{1,0:T(8,128)(2,1)S(1)} collective-permute-done((bf16[128,2048]{1,0:T(8,128)(2,1)}, bf16[128,2048]{1,0:T(8,128)(2,1)S(1)}, u32[]{:S(2)}, u32[]{:S(2)}) %collective-permute-start.22) | collective-permute-done | bytes 524320 | tf_op jit(solution)/shard_map/ppermute | solution.py:313
  347.3 1.3 collective-permute-start.26
  349.6 1.2 fusion.12
  350.9 1.2 fusion.15
  352.1 6.1 %collective-permute-done.24 = bf16[128,2048]{1,0:T(8,128)(2,1)S(1)} collective-permute-done((bf16[128,2048]{1,0:T(8,128)(2,1)}, bf16[128,2048]{1,0:T(8,128)(2,1)S(1)}, u32[]{:S(2)}, u32[]{:S(2)}) %collective-permute-start.24) | collective-permute-done | bytes 524320 | tf_op jit(solution)/shard_map/ppermute | solution.py:313
  358.2 2.5 collective-permute-start.30
  360.7 8.0 %collective-permute-done.25 = bf16[128,2048]{1,0:T(8,128)(2,1)S(1)} collective-permute-done((bf16[128,2048]{1,0:T(8,128)(2,1)}, bf16[128,2048]{1,0:T(8,128)(2,1)S(1)}, u32[]{:S(2)}, u32[]{:S(2)}) %collective-permute-start.25) | collective-permute-done | bytes 524320 | tf_op jit(solution)/shard_map/ppermute | solution.py:313
  368.7 1.1 collective-permute-done.26
  369.9 1.9 collective-permute-start.36
  371.8 1.4 add_convert_fusion
  373.2 1.1 pad_maximum_fusion
  374.2 1.3 collective-permute-start.38
  376.1 2.8 collective-permute-start.32
  378.9 1.3 collective-permute-start.34
  380.4 1.0 fusion.11
  382.4 8.3 %collective-permute-done.37 = bf16[64,1024]{1,0:T(8,128)(2,1)S(1)} collective-permute-done((bf16[64,1024]{1,0:T(8,128)(2,1)S(1)}, bf16[64,1024]{1,0:T(8,128)(2,1)S(1)}, u32[]{:S(2)}, u32[]{:S(2)}) %collective-permute-start.37) | collective-permute-done | bytes 131104 | tf_op jit(solution)/shard_map/ppermute | solution.py:313
  390.7 1.0 fusion.8
  391.7 4.8 %collective-permute-done.34 = bf16[64,2048]{1,0:T(8,128)(2,1)S(1)} collective-permute-done((bf16[64,2048]{1,0:T(8,128)(2,1)S(1)}, bf16[64,2048]{1,0:T(8,128)(2,1)S(1)}, u32[]{:S(2)}, u32[]{:S(2)}) %collective-permute-start.34) | collective-permute-done | bytes 262176 | tf_op jit(solution)/shard_map/ppermute | solution.py:313
  396.5 13.1 %collective-permute-done.33 = bf16[64,2048]{1,0:T(8,128)(2,1)S(1)} collective-permute-done((bf16[64,2048]{1,0:T(8,128)(2,1)S(1)}, bf16[64,2048]{1,0:T(8,128)(2,1)S(1)}, u32[]{:S(2)}, u32[]{:S(2)}) %collective-permute-start.33) | collective-permute-done | bytes 262176 | tf_op jit(solution)/shard_map/ppermute | solution.py:313
  (118 shorter events, 17.4 us)
Async XLA Ops:
  12.1 12.0 %collective-permute-start.13 = (f32[1,4096]{1,0:T(1,128)S(1)}, f32[1,4096]{1,0:T(1,128)}, u32[]{:S(2)}, u32[]{:S(2)}) collective-permute-start(f32[1,4096]{1,0:T(1,128)S(1)} %bitcast.47), channel_id=1, source_target_pairs={{0,24},{8,16},{16,8},{24,0},{1,25},{9,17},{17,9},{25,1},{2,26},{10... | collective-permute-start | bytes 49160 | tf_op jit(solution)/shard_map/ppermute | solution.py:313
  16.1 11.7 %collective-permute-start.12 = (f32[1,4096]{1,0:T(1,128)S(1)}, f32[1,4096]{1,0:T(1,128)}, u32[]{:S(2)}, u32[]{:S(2)}) collective-permute-start(f32[1,4096]{1,0:T(1,128)S(1)} %bitcast.48), channel_id=1, source_target_pairs={{0,16},{8,24},{16,0},{24,8},{1,17},{9,25},{17,1},{25,9},{2,18},{10... | collective-permute-start | bytes 49160 | tf_op jit(solution)/shard_map/ppermute | solution.py:313
  16.6 11.2 %collective-permute-start.11 = (f32[1,4096]{1,0:T(1,128)S(1)}, f32[1,4096]{1,0:T(1,128)}, u32[]{:S(2)}, u32[]{:S(2)}) collective-permute-start(f32[1,4096]{1,0:T(1,128)S(1)} %bitcast.49), channel_id=1, source_target_pairs={{0,8},{8,0},{16,24},{24,16},{1,9},{9,1},{17,25},{25,17},{2,10},{10... | collective-permute-start | bytes 49160 | tf_op jit(solution)/shard_map/ppermute | solution.py:313
  16.7 24.5 %collective-permute-start.8 = (bf16[128,4096]{1,0:T(8,128)(2,1)S(1)}, bf16[128,4096]{1,0:T(8,128)(2,1)S(1)}, u32[]{:S(2)}, u32[]{:S(2)}) collective-permute-start(bf16[128,4096]{1,0:T(8,128)(2,1)S(1)} %copy-done.2), channel_id=1, source_target_pairs={{0,16},{8,24},{16,0},{24,8},{1,17},{9,25},{17,1},{25,9},{2,18},{10... | collective-permute-start | bytes 3145736 | tf_op jit(solution)/shard_map/ppermute | solution.py:313
  18.6 26.0 %collective-permute-start.7 = (bf16[128,4096]{1,0:T(8,128)(2,1)S(1)}, bf16[128,4096]{1,0:T(8,128)(2,1)S(1)}, u32[]{:S(2)}, u32[]{:S(2)}) collective-permute-start(bf16[128,4096]{1,0:T(8,128)(2,1)S(1)} %copy-done.2), channel_id=1, source_target_pairs={{0,8},{8,0},{16,24},{24,16},{1,9},{9,1},{17,25},{25,17},{2,10},{10... | collective-permute-start | bytes 3145736 | tf_op jit(solution)/shard_map/ppermute | solution.py:313
  24.1 125.4 %copy-start.3 = (bf16[64,3072]{1,0:T(8,128)(2,1)}, bf16[64,3072]{1,0:T(8,128)(2,1)S(1)}, u32[]{:S(2)}) copy-start(bf16[64,3072]{1,0:T(8,128)(2,1)S(1)} %slice.105.refs_0_) | copy-start | bytes 1179652
  24.1 25.5 %collective-permute-start.19 = (bf16[64,1024]{1,0:T(8,128)(2,1)}, bf16[64,1024]{1,0:T(8,128)(2,1)}, u32[]{:S(2)}, u32[]{:S(2)}) collective-permute-start(bf16[64,1024]{1,0:T(8,128)(2,1)} %slice.111.refs_0_), channel_id=1, source_target_pairs={{0,6},{1,7},{2,4},{3,5},{4,2},{5,3},{6,0},{7,1},{8,14},{9,15},{10,... | collective-permute-start | bytes 393224 | tf_op jit(solution)/shard_map/ppermute | solution.py:313
  27.8 29.9 %collective-permute-start.17 = (bf16[64,1024]{1,0:T(8,128)(2,1)}, bf16[64,1024]{1,0:T(8,128)(2,1)}, u32[]{:S(2)}, u32[]{:S(2)}) collective-permute-start(bf16[64,1024]{1,0:T(8,128)(2,1)} %slice.111.refs_0_), channel_id=1, source_target_pairs={{0,4},{1,5},{2,6},{3,7},{4,0},{5,1},{6,2},{7,3},{8,12},{9,13},{10,... | collective-permute-start | bytes 393224 | tf_op jit(solution)/shard_map/ppermute | solution.py:313
  27.8 33.3 %collective-permute-start.15 = (bf16[64,1024]{1,0:T(8,128)(2,1)}, bf16[64,1024]{1,0:T(8,128)(2,1)}, u32[]{:S(2)}, u32[]{:S(2)}) collective-permute-start(bf16[64,1024]{1,0:T(8,128)(2,1)} %slice.111.refs_0_), channel_id=1, source_target_pairs={{0,2},{1,3},{2,0},{3,1},{4,6},{5,7},{6,4},{7,5},{8,10},{9,11},{10,... | collective-permute-start | bytes 393224 | tf_op jit(solution)/shard_map/ppermute | solution.py:313
  43.0 12.7 %collective-permute-start.9 = (bf16[64,4096]{1,0:T(8,128)(2,1)}, bf16[64,4096]{1,0:T(8,128)(2,1)}, u32[]{:S(2)}, u32[]{:S(2)}) collective-permute-start(bf16[64,4096]{1,0:T(8,128)(2,1)} %slice.139), channel_id=1, source_target_pairs={{0,8},{8,0},{16,24},{24,16},{1,9},{9,1},{17,25},{25,17},{2,10},{10... | collective-permute-start | bytes 1572872 | tf_op jit(solution)/shard_map/ppermute | solution.py:313
  45.6 16.4 %collective-permute-start.10 = (bf16[64,4096]{1,0:T(8,128)(2,1)S(1)}, bf16[64,4096]{1,0:T(8,128)(2,1)S(1)}, u32[]{:S(2)}, u32[]{:S(2)}) collective-permute-start(bf16[64,4096]{1,0:T(8,128)(2,1)S(1)} %slice.140), channel_id=1, source_target_pairs={{0,16},{8,24},{16,0},{24,8},{1,17},{9,25},{17,1},{25,9},{2,18},{10... | collective-permute-start | bytes 1572872 | tf_op jit(solution)/shard_map/ppermute | solution.py:313
  49.6 11.5 %collective-permute-start.14 = (bf16[64,1024]{1,0:T(8,128)(2,1)}, bf16[64,1024]{1,0:T(8,128)(2,1)S(1)}, u32[]{:S(2)}, u32[]{:S(2)}) collective-permute-start(bf16[64,1024]{1,0:T(8,128)(2,1)} %slice.111.refs_0_), channel_id=1, source_target_pairs={{0,1},{1,0},{2,3},{3,2},{4,5},{5,4},{6,7},{7,6},{8,9},{9,8},{10,11... | collective-permute-start | bytes 393224 | tf_op jit(solution)/shard_map/ppermute | solution.py:313
  55.8 6.3 %collective-permute-start.20 = (bf16[64,1024]{1,0:T(8,128)(2,1)}, bf16[64,1024]{1,0:T(8,128)(2,1)S(1)}, u32[]{:S(2)}, u32[]{:S(2)}) collective-permute-start(bf16[64,1024]{1,0:T(8,128)(2,1)} %collective-permute-done.19.refs_6_), channel_id=1, source_target_pairs={{0,1},{1,0},{2,3},{3,2},{4,5},{5,4},{6,7},{7,6},{8,9},{9,8},{10,11... | collective-permute-start | bytes 393224 | tf_op jit(solution)/shard_map/ppermute | solution.py:313
  57.7 13.9 %collective-permute-start.5 = (bf16[64,3072]{1,0:T(8,128)(2,1)S(1)}, bf16[64,3072]{1,0:T(8,128)(2,1)S(1)}, u32[]{:S(2)}, u32[]{:S(2)}) collective-permute-start(bf16[64,3072]{1,0:T(8,128)(2,1)S(1)} %slice.105.refs_0_), channel_id=1, source_target_pairs={{0,6},{1,7},{2,4},{3,5},{4,2},{5,3},{6,0},{7,1},{8,14},{9,15},{10,... | collective-permute-start | bytes 1179656 | tf_op jit(solution)/shard_map/ppermute | solution.py:313
  61.1 34.3 %collective-permute-start.3 = (bf16[64,3072]{1,0:T(8,128)(2,1)S(1)}, bf16[64,3072]{1,0:T(8,128)(2,1)}, u32[]{:S(2)}, u32[]{:S(2)}) collective-permute-start(bf16[64,3072]{1,0:T(8,128)(2,1)S(1)} %slice.105.refs_0_), channel_id=1, source_target_pairs={{0,4},{1,5},{2,6},{3,7},{4,0},{5,1},{6,2},{7,3},{8,12},{9,13},{10,... | collective-permute-start | bytes 1179656 | tf_op jit(solution)/shard_map/ppermute | solution.py:313
  61.1 34.3 %copy-start.20 = (bf16[64,1024]{1,0:T(8,128)(2,1)}, bf16[64,1024]{1,0:T(8,128)(2,1)S(1)}, u32[]{:S(2)}) copy-start(bf16[64,1024]{1,0:T(8,128)(2,1)S(1)} %collective-permute-done.14.refs_1_) | copy-start | bytes 393220
  61.1 34.3 %collective-permute-start.1 = (bf16[64,3072]{1,0:T(8,128)(2,1)S(1)}, bf16[64,3072]{1,0:T(8,128)(2,1)}, u32[]{:S(2)}, u32[]{:S(2)}) collective-permute-start(bf16[64,3072]{1,0:T(8,128)(2,1)S(1)} %slice.105.refs_0_), channel_id=1, source_target_pairs={{0,2},{1,3},{2,0},{3,1},{4,6},{5,7},{6,4},{7,5},{8,10},{9,11},{10,... | collective-permute-start | bytes 1179656 | tf_op jit(solution)/shard_map/ppermute | solution.py:313
  62.1 33.9 %copy-start.21 = (bf16[64,1024]{1,0:T(8,128)(2,1)}, bf16[64,1024]{1,0:T(8,128)(2,1)S(1)}, u32[]{:S(2)}) copy-start(bf16[64,1024]{1,0:T(8,128)(2,1)S(1)} %collective-permute-done.20.refs_7_) | copy-start | bytes 393220
  62.1 1.6 collective-permute-start.18
  62.1 33.9 %collective-permute-start.16 = (bf16[64,1024]{1,0:T(8,128)(2,1)}, bf16[64,1024]{1,0:T(8,128)(2,1)}, u32[]{:S(2)}, u32[]{:S(2)}) collective-permute-start(bf16[64,1024]{1,0:T(8,128)(2,1)} %collective-permute-done.15.refs_2_), channel_id=1, source_target_pairs={{0,1},{1,0},{2,3},{3,2},{4,5},{5,4},{6,7},{7,6},{8,9},{9,8},{10,11... | collective-permute-start | bytes 393224 | tf_op jit(solution)/shard_map/ppermute | solution.py:313
  63.6 85.9 %collective-permute-start = (bf16[64,3072]{1,0:T(8,128)(2,1)S(1)}, bf16[64,3072]{1,0:T(8,128)(2,1)}, u32[]{:S(2)}, u32[]{:S(2)}) collective-permute-start(bf16[64,3072]{1,0:T(8,128)(2,1)S(1)} %slice.105.refs_0_), channel_id=1, source_target_pairs={{0,1},{1,0},{2,3},{3,2},{4,5},{5,4},{6,7},{7,6},{8,9},{9,8},{10,11... | collective-permute-start | bytes 1179656 | tf_op jit(solution)/shard_map/ppermute | solution.py:313
  71.6 77.9 %copy-start.7 = (bf16[64,3072]{1,0:T(8,128)(2,1)}, bf16[64,3072]{1,0:T(8,128)(2,1)S(1)}, u32[]{:S(2)}) copy-start(bf16[64,3072]{1,0:T(8,128)(2,1)S(1)} %collective-permute-done.5.refs_6_) | copy-start | bytes 1179652
  71.6 77.9 %collective-permute-start.6 = (bf16[64,3072]{1,0:T(8,128)(2,1)S(1)}, bf16[64,3072]{1,0:T(8,128)(2,1)}, u32[]{:S(2)}, u32[]{:S(2)}) collective-permute-start(bf16[64,3072]{1,0:T(8,128)(2,1)S(1)} %collective-permute-done.5.refs_6_), channel_id=1, source_target_pairs={{0,1},{1,0},{2,3},{3,2},{4,5},{5,4},{6,7},{7,6},{8,9},{9,8},{10,11... | collective-permute-start | bytes 1179656 | tf_op jit(solution)/shard_map/ppermute | solution.py:313
  95.4 54.1 %collective-permute-start.4 = (bf16[64,3072]{1,0:T(8,128)(2,1)}, bf16[64,3072]{1,0:T(8,128)(2,1)}, u32[]{:S(2)}, u32[]{:S(2)}) collective-permute-start(bf16[64,3072]{1,0:T(8,128)(2,1)} %collective-permute-done.3.refs_4_), channel_id=1, source_target_pairs={{0,1},{1,0},{2,3},{3,2},{4,5},{5,4},{6,7},{7,6},{8,9},{9,8},{10,11... | collective-permute-start | bytes 1179656 | tf_op jit(solution)/shard_map/ppermute | solution.py:313
  95.4 54.1 %collective-permute-start.2 = (bf16[64,3072]{1,0:T(8,128)(2,1)}, bf16[64,3072]{1,0:T(8,128)(2,1)}, u32[]{:S(2)}, u32[]{:S(2)}) collective-permute-start(bf16[64,3072]{1,0:T(8,128)(2,1)} %collective-permute-done.1.refs_2_), channel_id=1, source_target_pairs={{0,1},{1,0},{2,3},{3,2},{4,5},{5,4},{6,7},{7,6},{8,9},{9,8},{10,11... | collective-permute-start | bytes 1179656 | tf_op jit(solution)/shard_map/ppermute | solution.py:313
  282.9 65.8 %copy-start.10 = (bf16[128,2048]{1,0:T(8,128)(2,1)S(1)}, bf16[128,2048]{1,0:T(8,128)(2,1)}, u32[]{:S(2)}) copy-start(bf16[128,2048]{1,0:T(8,128)(2,1)} %get-tuple-element.35) | copy-start | bytes 1572868
  314.9 60.7 %copy-start.6 = (f32[4,64,2048]{2,1,0:T(8,128)S(1)}, f32[4,64,2048]{2,1,0:T(8,128)}, u32[]{:S(2)}) copy-start(f32[4,64,2048]{2,1,0:T(8,128)} %get-tuple-element.47) | copy-start | bytes 6291460
  316.9 5.0 %collective-permute-start.40 = (f32[3,4096]{1,0:T(4,128)S(1)}, f32[3,4096]{1,0:T(4,128)S(1)}, u32[]{:S(2)}, u32[]{:S(2)}) collective-permute-start(f32[3,4096]{1,0:T(4,128)S(1)} %fusion.20), channel_id=1, source_target_pairs={{0,16},{8,24},{16,0},{24,8},{1,17},{9,25},{17,1},{25,9},{2,18},{10... | collective-permute-start | bytes 147464 | tf_op jit(solution)/shard_map/ppermute | solution.py:313
  318.3 5.7 %collective-permute-start.41 = (f32[3,4096]{1,0:T(4,128)S(1)}, f32[3,4096]{1,0:T(4,128)S(1)}, u32[]{:S(2)}, u32[]{:S(2)}) collective-permute-start(f32[3,4096]{1,0:T(4,128)S(1)} %fusion.20), channel_id=1, source_target_pairs={{0,24},{8,16},{16,8},{24,0},{1,25},{9,17},{17,9},{25,1},{2,26},{10... | collective-permute-start | bytes 147464 | tf_op jit(solution)/shard_map/ppermute | solution.py:313
  319.9 5.4 %collective-permute-start.39 = (f32[3,4096]{1,0:T(4,128)S(1)}, f32[3,4096]{1,0:T(4,128)S(1)}, u32[]{:S(2)}, u32[]{:S(2)}) collective-permute-start(f32[3,4096]{1,0:T(4,128)S(1)} %fusion.20), channel_id=1, source_target_pairs={{0,8},{8,0},{16,24},{24,16},{1,9},{9,1},{17,25},{25,17},{2,10},{10... | collective-permute-start | bytes 147464 | tf_op jit(solution)/shard_map/ppermute | solution.py:313
  320.4 28.6 %collective-permute-start.27 = (bf16[4,64,1024]{2,1,0:T(8,128)(2,1)}, bf16[4,64,1024]{2,1,0:T(8,128)(2,1)S(1)}, u32[]{:S(2)}, u32[]{:S(2)}) collective-permute-start(bf16[4,64,1024]{2,1,0:T(8,128)(2,1)} %get-tuple-element.46), channel_id=1, source_target_pairs={{0,1},{1,0},{2,3},{3,2},{4,5},{5,4},{6,7},{7,6},{8,9},{9,8},{10,11... | collective-permute-start | bytes 1572872 | tf_op jit(solution)/shard_map/ppermute | solution.py:313
  320.4 15.3 %collective-permute-start.21 = (bf16[128,2048]{1,0:T(8,128)(2,1)}, bf16[128,2048]{1,0:T(8,128)(2,1)S(1)}, u32[]{:S(2)}, u32[]{:S(2)}) collective-permute-start(bf16[128,2048]{1,0:T(8,128)(2,1)} %get-tuple-element.36), channel_id=1, source_target_pairs={{0,8},{8,0},{16,24},{24,16},{1,9},{9,1},{17,25},{25,17},{2,10},{10... | collective-permute-start | bytes 1572872 | tf_op jit(solution)/shard_map/ppermute | solution.py:313
  321.9 25.5 %collective-permute-start.22 = (bf16[128,2048]{1,0:T(8,128)(2,1)}, bf16[128,2048]{1,0:T(8,128)(2,1)S(1)}, u32[]{:S(2)}, u32[]{:S(2)}) collective-permute-start(bf16[128,2048]{1,0:T(8,128)(2,1)} %get-tuple-element.37), channel_id=1, source_target_pairs={{0,16},{8,24},{16,0},{24,8},{1,17},{9,25},{17,1},{25,9},{2,18},{10... | collective-permute-start | bytes 1572872 | tf_op jit(solution)/shard_map/ppermute | solution.py:313
  324.0 24.7 %collective-permute-start.23 = (bf16[128,2048]{1,0:T(8,128)(2,1)}, bf16[128,2048]{1,0:T(8,128)(2,1)S(1)}, u32[]{:S(2)}, u32[]{:S(2)}) collective-permute-start(bf16[128,2048]{1,0:T(8,128)(2,1)} %get-tuple-element.38), channel_id=1, source_target_pairs={{0,24},{8,16},{16,8},{24,0},{1,25},{9,17},{17,9},{25,1},{2,26},{10... | collective-permute-start | bytes 1572872 | tf_op jit(solution)/shard_map/ppermute | solution.py:313
  325.2 33.0 %collective-permute-start.24 = (bf16[128,2048]{1,0:T(8,128)(2,1)}, bf16[128,2048]{1,0:T(8,128)(2,1)S(1)}, u32[]{:S(2)}, u32[]{:S(2)}) collective-permute-start(bf16[128,2048]{1,0:T(8,128)(2,1)} %get-tuple-element.42), channel_id=1, source_target_pairs={{0,8},{8,0},{16,24},{24,16},{1,9},{9,1},{17,25},{25,17},{2,10},{10... | collective-permute-start | bytes 1572872 | tf_op jit(solution)/shard_map/ppermute | solution.py:313
  335.7 33.0 %collective-permute-start.25 = (bf16[128,2048]{1,0:T(8,128)(2,1)}, bf16[128,2048]{1,0:T(8,128)(2,1)S(1)}, u32[]{:S(2)}, u32[]{:S(2)}) collective-permute-start(bf16[128,2048]{1,0:T(8,128)(2,1)} %get-tuple-element.43), channel_id=1, source_target_pairs={{0,16},{8,24},{16,0},{24,8},{1,17},{9,25},{17,1},{25,9},{2,18},{10... | collective-permute-start | bytes 1572872 | tf_op jit(solution)/shard_map/ppermute | solution.py:313
  347.3 22.5 %collective-permute-start.26 = (bf16[128,2048]{1,0:T(8,128)(2,1)}, bf16[128,2048]{1,0:T(8,128)(2,1)S(1)}, u32[]{:S(2)}, u32[]{:S(2)}) collective-permute-start(bf16[128,2048]{1,0:T(8,128)(2,1)} %get-tuple-element.44), channel_id=1, source_target_pairs={{0,24},{8,16},{16,8},{24,0},{1,25},{9,17},{17,9},{25,1},{2,26},{10... | collective-permute-start | bytes 1572872 | tf_op jit(solution)/shard_map/ppermute | solution.py:313
  348.7 2.1 collective-permute-start.35
  349.0 25.2 %collective-permute-start.31 = (bf16[4,64,2048]{2,1,0:T(8,128)(2,1)}, bf16[4,64,2048]{2,1,0:T(8,128)(2,1)S(1)}, u32[]{:S(2)}, u32[]{:S(2)}) collective-permute-start(bf16[4,64,2048]{2,1,0:T(8,128)(2,1)} %get-tuple-element.48), channel_id=1, source_target_pairs={{0,1},{1,0},{2,3},{3,2},{4,5},{5,4},{6,7},{7,6},{8,9},{9,8},{10,11... | collective-permute-start | bytes 3145736 | tf_op jit(solution)/shard_map/ppermute | solution.py:313
  350.8 25.0 %collective-permute-start.28 = (bf16[64,1024]{1,0:T(8,128)(2,1)S(1)}, bf16[64,1024]{1,0:T(8,128)(2,1)S(1)}, u32[]{:S(2)}, u32[]{:S(2)}) collective-permute-start(bf16[64,1024]{1,0:T(8,128)(2,1)S(1)} %get-tuple-element.65), channel_id=1, source_target_pairs={{0,2},{1,3},{2,0},{3,1},{4,6},{5,7},{6,4},{7,5},{8,10},{9,11},{10,... | collective-permute-start | bytes 393224 | tf_op jit(solution)/shard_map/ppermute | solution.py:313
  358.2 17.8 %collective-permute-start.30 = (bf16[64,1024]{1,0:T(8,128)(2,1)S(1)}, bf16[64,1024]{1,0:T(8,128)(2,1)S(1)}, u32[]{:S(2)}, u32[]{:S(2)}) collective-permute-start(bf16[64,1024]{1,0:T(8,128)(2,1)S(1)} %get-tuple-element.66), channel_id=1, source_target_pairs={{0,6},{1,7},{2,4},{3,5},{4,2},{5,3},{6,0},{7,1},{8,14},{9,15},{10,... | collective-permute-start | bytes 393224 | tf_op jit(solution)/shard_map/ppermute | solution.py:313
  368.7 10.1 %collective-permute-start.29 = (bf16[64,1024]{1,0:T(8,128)(2,1)S(1)}, bf16[64,1024]{1,0:T(8,128)(2,1)S(1)}, u32[]{:S(2)}, u32[]{:S(2)}) collective-permute-start(bf16[64,1024]{1,0:T(8,128)(2,1)S(1)} %get-tuple-element.67), channel_id=1, source_target_pairs={{0,4},{1,5},{2,6},{3,7},{4,0},{5,1},{6,2},{7,3},{8,12},{9,13},{10,... | collective-permute-start | bytes 393224 | tf_op jit(solution)/shard_map/ppermute | solution.py:313
  369.9 10.4 %collective-permute-start.36 = (bf16[64,1024]{1,0:T(8,128)(2,1)S(1)}, bf16[64,1024]{1,0:T(8,128)(2,1)S(1)}, u32[]{:S(2)}, u32[]{:S(2)}) collective-permute-start(bf16[64,1024]{1,0:T(8,128)(2,1)S(1)} %get-tuple-element.68), channel_id=1, source_target_pairs={{0,2},{1,3},{2,0},{3,1},{4,6},{5,7},{6,4},{7,5},{8,10},{9,11},{10,... | collective-permute-start | bytes 393224 | tf_op jit(solution)/shard_map/ppermute | solution.py:313
  374.2 8.2 %collective-permute-start.38 = (bf16[64,1024]{1,0:T(8,128)(2,1)S(1)}, bf16[64,1024]{1,0:T(8,128)(2,1)S(1)}, u32[]{:S(2)}, u32[]{:S(2)}) collective-permute-start(bf16[64,1024]{1,0:T(8,128)(2,1)S(1)} %get-tuple-element.69), channel_id=1, source_target_pairs={{0,6},{1,7},{2,4},{3,5},{4,2},{5,3},{6,0},{7,1},{8,14},{9,15},{10,... | collective-permute-start | bytes 393224 | tf_op jit(solution)/shard_map/ppermute | solution.py:313
  375.8 14.9 %collective-permute-start.37 = (bf16[64,1024]{1,0:T(8,128)(2,1)S(1)}, bf16[64,1024]{1,0:T(8,128)(2,1)S(1)}, u32[]{:S(2)}, u32[]{:S(2)}) collective-permute-start(bf16[64,1024]{1,0:T(8,128)(2,1)S(1)} %get-tuple-element.70), channel_id=1, source_target_pairs={{0,4},{1,5},{2,6},{3,7},{4,0},{5,1},{6,2},{7,3},{8,12},{9,13},{10,... | collective-permute-start | bytes 393224 | tf_op jit(solution)/shard_map/ppermute | solution.py:313
  376.1 15.6 %collective-permute-start.32 = (bf16[64,2048]{1,0:T(8,128)(2,1)S(1)}, bf16[64,2048]{1,0:T(8,128)(2,1)S(1)}, u32[]{:S(2)}, u32[]{:S(2)}) collective-permute-start(bf16[64,2048]{1,0:T(8,128)(2,1)S(1)} %get-tuple-element.62), channel_id=1, source_target_pairs={{0,2},{1,3},{2,0},{3,1},{4,6},{5,7},{6,4},{7,5},{8,10},{9,11},{10,... | collective-permute-start | bytes 786440 | tf_op jit(solution)/shard_map/ppermute | solution.py:313
  378.9 17.7 %collective-permute-start.34 = (bf16[64,2048]{1,0:T(8,128)(2,1)S(1)}, bf16[64,2048]{1,0:T(8,128)(2,1)S(1)}, u32[]{:S(2)}, u32[]{:S(2)}) collective-permute-start(bf16[64,2048]{1,0:T(8,128)(2,1)S(1)} %get-tuple-element.63), channel_id=1, source_target_pairs={{0,6},{1,7},{2,4},{3,5},{4,2},{5,3},{6,0},{7,1},{8,14},{9,15},{10,... | collective-permute-start | bytes 786440 | tf_op jit(solution)/shard_map/ppermute | solution.py:313
  380.2 29.4 %collective-permute-start.33 = (bf16[64,2048]{1,0:T(8,128)(2,1)S(1)}, bf16[64,2048]{1,0:T(8,128)(2,1)S(1)}, u32[]{:S(2)}, u32[]{:S(2)}) collective-permute-start(bf16[64,2048]{1,0:T(8,128)(2,1)S(1)} %get-tuple-element.64), channel_id=1, source_target_pairs={{0,4},{1,5},{2,6},{3,7},{4,0},{5,1},{6,2},{7,3},{8,12},{9,13},{10,... | collective-permute-start | bytes 786440 | tf_op jit(solution)/shard_map/ppermute | solution.py:313
  (17 other events, 366.4 us)
where the time goes:
time: 411 us
  Pallas kernels  219 us (53%)
  waiting for transfers between devices  111 us (27%)
  starting transfers between devices  43.1 us (10%)
  other arithmetic  26.5 us (6%)
  local copies, waits for them, and re-layouts  9.8 us (2%)
    pallas_call x4, Pallas kernels, main_call(): pl.pallas_call(functools.partial(main_kernel, nrow=nrow, ncol=ncol, nd=nd...  219 us
    ppermute x42, waiting for transfers between devices, swap(): return lax.ppermute(value, axis, [(i, i ^ k) for i in range(size)])  111 us
    ppermute x42, starting transfers between devices, swap(): return lax.ppermute(value, axis, [(i, i ^ k) for i in range(size)])  43.1 us
    reduce_max x1, other arithmetic, layer(): peak = jnp.max(jnp.abs(weight), axis=0, keepdims=True).astype(f32)  11.4 us
  transfers between devices with their start and end apart: 42, of which 15 were waited for; matrix products, arithmetic and copies ran while one was open for 5% of the time, Pallas kernels for 13%

commit v1 on v0

--- a/solution.py
+++ b/solution.py
@@ -235,7 +235,7 @@
                     ins[1][k, :, cols] = in_acc[d, pl.ds(other, rows_t), :].astype(jnp.bfloat16)
 
 
-def main_call(meta, toks, cots, weight, consts, wg, out_prev, in_prev, *, rows, t0, cols, final, bd=256, bj=512, strip=16):
+def main_call(meta, toks, cots, weight, consts, wg, out_prev, in_prev, *, rows, t0, cols, final, bd=512, bj=512, strip=32):
     nrow, ncol = len(cots), len(toks)
     nz = ncol // 2
     (d0, depth), (j0, width) = rows, cols
@@ -377,7 +377,8 @@
             keep, send = res
             got = swap(send, "col", ncol, 1)
             sums = [keep[k] + got[k].astype(f32) for k in range(nz)]
-            far = [swap(sums[k].astype(bf), "col", ncol, 2 * k) for k in range(1, nz)]
+            halves = [x.astype(bf) for x in sums]
+            far = [swap(halves[k], "col", ncol, 2 * k) for k in range(1, nz)]
             inputs.append(sum([sums[0]] + [x.astype(f32) for x in far]).astype(bf))
     mixed_out = jnp.concatenate(mixed, axis=1)
     input_grad = jnp.concatenate(inputs, axis=1)
@@ -386,7 +387,8 @@
     sines = jnp.concatenate([scale[n] * parts[n : n + 1] for n in range(3)], axis=0)
     common = jnp.concatenate(commons, axis=1) + jnp.sum(shares * sines, axis=0, keepdims=True)
     terms = common - sines
-    terms = sum([terms] + [swap(terms, "row", nrow, k) for k in range(1, nrow)])
+    far = [swap(terms, "row", nrow, k) for k in range(1, nrow)]
+    terms = sum([terms] + far)
     logit_grad = shares * (terms - jnp.sum(shares * terms, axis=0, keepdims=True))
     return mixed_out, input_grad, wg, logit_grad
 

time: 411 us -> 400 us (0.973)
  Pallas kernels: 219 us -> 208 us
    pallas_call x4, Pallas kernels: 219 us -> 208 us  [main_call(): pl.pallas_call(functools.partial(main_kernel, nrow=nrow, ncol=ncol, nd=nd...]
where the time goes in v1:
time: 400 us
  Pallas kernels  208 us (52%)
  waiting for transfers between devices  111 us (28%)
  starting transfers between devices  43.1 us (11%)
  other arithmetic  26.5 us (7%)
  local copies, waits for them, and re-layouts  9.8 us (2%)
    pallas_call x4, Pallas kernels, main_call(): pl.pallas_call(functools.partial(main_kernel, nrow=nrow, ncol=ncol, nd=nd...  208 us
    ppermute x42, waiting for transfers between devices, swap(): return lax.ppermute(value, axis, [(i, i ^ k) for i in range(size)])  111 us
    ppermute x42, starting transfers between devices, swap(): return lax.ppermute(value, axis, [(i, i ^ k) for i in range(size)])  43.1 us
    reduce_max x1, other arithmetic, layer(): peak = jnp.max(jnp.abs(weight), axis=0, keepdims=True).astype(f32)  11.4 us
  transfers between devices with their start and end apart: 42, of which 15 were waited for; matrix products, arithmetic and copies ran while one was open for 5% of the time, Pallas kernels for 13%

profile of v1, /device:TPU:0, one launch (start us, length us, event | category | flops | bytes accessed | tf_op | source)
XLA Modules:
  0.0 399.7 jit_solution(11741960378719259175)
XLA Ops:
  0.7 11.4 %abs_reduce_fusion = bf16[4096]{0:T(1024)(128)(2,1)S(1)} fusion(bf16[4096,4096]{1,0:T(8,128)(2,1)} %refs_12_.7), kind=kLoop, calls=%fused_computation | loop fusion | flops 33550336 | bytes 33562624 | tf_op jit(solution)/shard_map/reduce_max | solution.py:340
  12.1 4.0 collective-permute-start.13
  16.7 1.9 collective-permute-start.8
  18.6 1.5 collective-permute-start.7
  21.5 1.6 slice.111.refs_0_
  23.1 1.0 slice.105.refs_0_
  24.1 3.7 collective-permute-start.19
  28.6 1.7 slice_multiply_fusion.3
  30.3 11.0 %collective-permute-done.8.refs_10_ = bf16[128,4096]{1,0:T(8,128)(2,1)S(1)} collective-permute-done((bf16[128,4096]{1,0:T(8,128)(2,1)S(1)}, bf16[128,4096]{1,0:T(8,128)(2,1)S(1)}, u32[]{:S(2)}, u32[]{:S(2)}) %collective-permute-start.8) | collective-permute-done | bytes 1048608 | tf_op jit(solution)/shard_map/ppermute | solution.py:313
  43.0 1.6 collective-permute-start.9
  45.6 1.4 collective-permute-start.10
  48.1 1.6 concatenate.31.refs_13_
  49.7 6.1 %collective-permute-done.9 = bf16[64,4096]{1,0:T(8,128)(2,1)} collective-permute-done((bf16[64,4096]{1,0:T(8,128)(2,1)}, bf16[64,4096]{1,0:T(8,128)(2,1)}, u32[]{:S(2)}, u32[]{:S(2)}) %collective-permute-start.9) | collective-permute-done | bytes 524320 | tf_op jit(solution)/shard_map/ppermute | solution.py:313
  55.8 1.9 constant_dynamic-update-slice_fusion.1
  57.7 3.4 collective-permute-start.5
  63.8 7.8 %collective-permute-done.5.refs_6_ = bf16[64,3072]{1,0:T(8,128)(2,1)S(1)} collective-permute-done((bf16[64,3072]{1,0:T(8,128)(2,1)S(1)}, bf16[64,3072]{1,0:T(8,128)(2,1)S(1)}, u32[]{:S(2)}, u32[]{:S(2)}) %collective-permute-start.5) | collective-permute-done | bytes 393248 | tf_op jit(solution)/shard_map/ppermute | solution.py:313
  71.6 23.8 %collective-permute-done.3.refs_4_ = bf16[64,3072]{1,0:T(8,128)(2,1)} collective-permute-done((bf16[64,3072]{1,0:T(8,128)(2,1)S(1)}, bf16[64,3072]{1,0:T(8,128)(2,1)}, u32[]{:S(2)}, u32[]{:S(2)}) %collective-permute-start.3) | collective-permute-done | bytes 393248 | tf_op jit(solution)/shard_map/ppermute | solution.py:313
  96.0 50.7 %main_kernel.4 = (bf16[4096,4096]{1,0:T(8,128)(2,1)}, f32[3,4096]{1,0:T(4,128)}, f32[8,512,512]{2,1,0:T(8,128)}, f32[4,64,1024]{2,1,0:T(8,128)}, bf16[4,64,1024]{2,1,0:T(8,128)(2,1)}) custom-call(s32[2]{0:T(128)} %pad_add_fusion.meta, bf16[64,1024]{1,0:T(8,128)(2,1)} %slice.111.refs_0_, bf16[64,1024]{1,0:T(8,128)(2,1)} %copy-done.20, ...), custom_call_target="tpu_custom_call" | custom-call | flops 42949672960 | bytes 16777216 | tf_op jit(solution)/shard_map/main_kernel/pallas_call | solution.py:294
  146.8 95.7 %main_kernel.5 = (bf16[4096,4096]{1,0:T(8,128)(2,1)}, f32[3,4096]{1,0:T(4,128)}, f32[8,512,512]{2,1,0:T(8,128)}, f32[4,64,2048]{2,1,0:T(8,128)}, bf16[4,64,2048]{2,1,0:T(8,128)(2,1)}) custom-call(s32[2]{0:T(128)} %pad_add_fusion.meta, bf16[64,3072]{1,0:T(8,128)(2,1)} %copy-done.3, ...), custom_call_target="tpu_custom_call", output_to_operand_aliasing={{0}: (15, {})} | custom-call | flops 85899345920 | bytes 33554432 | tf_op jit(solution)/shard_map/main_kernel/pallas_call | solution.py:294
  242.5 30.3 %main_kernel.6 = (bf16[4096,4096]{1,0:T(8,128)(2,1)}, f32[3,2048]{1,0:T(4,128)}, bf16[128,2048]{1,0:T(8,128)(2,1)}, bf16[128,2048]{1,0:T(8,128)(2,1)}, bf16[128,...) custom-call(s32[2]{0:T(128)} %pad_add_fusion.meta, ...), custom_call_target="tpu_custom_call", output_to_operand_aliasing={{0}: (15, {})} | custom-call | flops 21474836480 | bytes 8388608 | tf_op jit(solution)/shard_map/main_kernel/pallas_call | solution.py:294
  272.9 31.1 %main_kernel.7 = (bf16[4096,4096]{1,0:T(8,128)(2,1)}, f32[3,2048]{1,0:T(4,128)}, bf16[128,2048]{1,0:T(8,128)(2,1)}, bf16[128,2048]{1,0:T(8,128)(2,1)}, bf16[128,...) custom-call(s32[2]{0:T(128)} %pad_add_fusion.meta, ...), custom_call_target="tpu_custom_call", output_to_operand_aliasing={{0}: (15, {})} | custom-call | flops 21474836480 | bytes 8388608 | tf_op jit(solution)/shard_map/main_kernel/pallas_call | solution.py:294
  306.0 1.4 collective-permute-start.40
  307.4 1.6 collective-permute-start.41
  309.6 1.4 collective-permute-start.21
  311.0 1.4 collective-permute-start.22
  313.1 1.2 collective-permute-start.23
  314.4 1.0 collective-permute-start.24
  316.2 8.6 %collective-permute-done.21 = bf16[128,2048]{1,0:T(8,128)(2,1)S(1)} collective-permute-done((bf16[128,2048]{1,0:T(8,128)(2,1)}, bf16[128,2048]{1,0:T(8,128)(2,1)S(1)}, u32[]{:S(2)}, u32[]{:S(2)}) %collective-permute-start.21) | collective-permute-done | bytes 524320 | tf_op jit(solution)/shard_map/ppermute | solution.py:313
  324.9 1.1 collective-permute-start.25
  325.9 10.5 %collective-permute-done.22 = bf16[128,2048]{1,0:T(8,128)(2,1)S(1)} collective-permute-done((bf16[128,2048]{1,0:T(8,128)(2,1)}, bf16[128,2048]{1,0:T(8,128)(2,1)S(1)}, u32[]{:S(2)}, u32[]{:S(2)}) %collective-permute-start.22) | collective-permute-done | bytes 524320 | tf_op jit(solution)/shard_map/ppermute | solution.py:313
  336.5 1.3 collective-permute-start.26
  338.7 1.2 fusion.12
  340.0 1.2 fusion.15
  341.2 6.1 %collective-permute-done.24 = bf16[128,2048]{1,0:T(8,128)(2,1)S(1)} collective-permute-done((bf16[128,2048]{1,0:T(8,128)(2,1)}, bf16[128,2048]{1,0:T(8,128)(2,1)S(1)}, u32[]{:S(2)}, u32[]{:S(2)}) %collective-permute-start.24) | collective-permute-done | bytes 524320 | tf_op jit(solution)/shard_map/ppermute | solution.py:313
  347.4 2.5 collective-permute-start.30
  349.8 8.0 %collective-permute-done.25 = bf16[128,2048]{1,0:T(8,128)(2,1)S(1)} collective-permute-done((bf16[128,2048]{1,0:T(8,128)(2,1)}, bf16[128,2048]{1,0:T(8,128)(2,1)S(1)}, u32[]{:S(2)}, u32[]{:S(2)}) %collective-permute-start.25) | collective-permute-done | bytes 524320 | tf_op jit(solution)/shard_map/ppermute | solution.py:313
  357.9 1.1 collective-permute-done.26
  359.0 1.9 collective-permute-start.36
  360.9 1.4 add_convert_fusion
  362.3 1.1 pad_maximum_fusion
  363.4 1.3 collective-permute-start.38
  365.2 2.8 collective-permute-start.32
  368.0 1.3 collective-permute-start.34
  369.5 1.0 fusion.11
  371.5 8.3 %collective-permute-done.37 = bf16[64,1024]{1,0:T(8,128)(2,1)S(1)} collective-permute-done((bf16[64,1024]{1,0:T(8,128)(2,1)S(1)}, bf16[64,1024]{1,0:T(8,128)(2,1)S(1)}, u32[]{:S(2)}, u32[]{:S(2)}) %collective-permute-start.37) | collective-permute-done | bytes 131104 | tf_op jit(solution)/shard_map/ppermute | solution.py:313
  379.8 1.0 fusion.8
  380.8 4.8 %collective-permute-done.34 = bf16[64,2048]{1,0:T(8,128)(2,1)S(1)} collective-permute-done((bf16[64,2048]{1,0:T(8,128)(2,1)S(1)}, bf16[64,2048]{1,0:T(8,128)(2,1)S(1)}, u32[]{:S(2)}, u32[]{:S(2)}) %collective-permute-start.34) | collective-permute-done | bytes 262176 | tf_op jit(solution)/shard_map/ppermute | solution.py:313
  385.7 13.1 %collective-permute-done.33 = bf16[64,2048]{1,0:T(8,128)(2,1)S(1)} collective-permute-done((bf16[64,2048]{1,0:T(8,128)(2,1)S(1)}, bf16[64,2048]{1,0:T(8,128)(2,1)S(1)}, u32[]{:S(2)}, u32[]{:S(2)}) %collective-permute-start.33) | collective-permute-done | bytes 262176 | tf_op jit(solution)/shard_map/ppermute | solution.py:313
  (118 shorter events, 17.4 us)
Async XLA Ops:
  12.1 12.0 %collective-permute-start.13 = (f32[1,4096]{1,0:T(1,128)S(1)}, f32[1,4096]{1,0:T(1,128)}, u32[]{:S(2)}, u32[]{:S(2)}) collective-permute-start(f32[1,4096]{1,0:T(1,128)S(1)} %bitcast.47), channel_id=1, source_target_pairs={{0,24},{8,16},{16,8},{24,0},{1,25},{9,17},{17,9},{25,1},{2,26},{10... | collective-permute-start | bytes 49160 | tf_op jit(solution)/shard_map/ppermute | solution.py:313
  16.1 11.7 %collective-permute-start.12 = (f32[1,4096]{1,0:T(1,128)S(1)}, f32[1,4096]{1,0:T(1,128)}, u32[]{:S(2)}, u32[]{:S(2)}) collective-permute-start(f32[1,4096]{1,0:T(1,128)S(1)} %bitcast.48), channel_id=1, source_target_pairs={{0,16},{8,24},{16,0},{24,8},{1,17},{9,25},{17,1},{25,9},{2,18},{10... | collective-permute-start | bytes 49160 | tf_op jit(solution)/shard_map/ppermute | solution.py:313
  16.6 11.2 %collective-permute-start.11 = (f32[1,4096]{1,0:T(1,128)S(1)}, f32[1,4096]{1,0:T(1,128)}, u32[]{:S(2)}, u32[]{:S(2)}) collective-permute-start(f32[1,4096]{1,0:T(1,128)S(1)} %bitcast.49), channel_id=1, source_target_pairs={{0,8},{8,0},{16,24},{24,16},{1,9},{9,1},{17,25},{25,17},{2,10},{10... | collective-permute-start | bytes 49160 | tf_op jit(solution)/shard_map/ppermute | solution.py:313
  16.7 24.5 %collective-permute-start.8 = (bf16[128,4096]{1,0:T(8,128)(2,1)S(1)}, bf16[128,4096]{1,0:T(8,128)(2,1)S(1)}, u32[]{:S(2)}, u32[]{:S(2)}) collective-permute-start(bf16[128,4096]{1,0:T(8,128)(2,1)S(1)} %copy-done.2), channel_id=1, source_target_pairs={{0,16},{8,24},{16,0},{24,8},{1,17},{9,25},{17,1},{25,9},{2,18},{10... | collective-permute-start | bytes 3145736 | tf_op jit(solution)/shard_map/ppermute | solution.py:313
  18.6 26.0 %collective-permute-start.7 = (bf16[128,4096]{1,0:T(8,128)(2,1)S(1)}, bf16[128,4096]{1,0:T(8,128)(2,1)S(1)}, u32[]{:S(2)}, u32[]{:S(2)}) collective-permute-start(bf16[128,4096]{1,0:T(8,128)(2,1)S(1)} %copy-done.2), channel_id=1, source_target_pairs={{0,8},{8,0},{16,24},{24,16},{1,9},{9,1},{17,25},{25,17},{2,10},{10... | collective-permute-start | bytes 3145736 | tf_op jit(solution)/shard_map/ppermute | solution.py:313
  24.1 122.6 %copy-start.3 = (bf16[64,3072]{1,0:T(8,128)(2,1)}, bf16[64,3072]{1,0:T(8,128)(2,1)S(1)}, u32[]{:S(2)}) copy-start(bf16[64,3072]{1,0:T(8,128)(2,1)S(1)} %slice.105.refs_0_) | copy-start | bytes 1179652
  24.1 25.5 %collective-permute-start.19 = (bf16[64,1024]{1,0:T(8,128)(2,1)}, bf16[64,1024]{1,0:T(8,128)(2,1)}, u32[]{:S(2)}, u32[]{:S(2)}) collective-permute-start(bf16[64,1024]{1,0:T(8,128)(2,1)} %slice.111.refs_0_), channel_id=1, source_target_pairs={{0,6},{1,7},{2,4},{3,5},{4,2},{5,3},{6,0},{7,1},{8,14},{9,15},{10,... | collective-permute-start | bytes 393224 | tf_op jit(solution)/shard_map/ppermute | solution.py:313
  27.8 29.9 %collective-permute-start.17 = (bf16[64,1024]{1,0:T(8,128)(2,1)}, bf16[64,1024]{1,0:T(8,128)(2,1)}, u32[]{:S(2)}, u32[]{:S(2)}) collective-permute-start(bf16[64,1024]{1,0:T(8,128)(2,1)} %slice.111.refs_0_), channel_id=1, source_target_pairs={{0,4},{1,5},{2,6},{3,7},{4,0},{5,1},{6,2},{7,3},{8,12},{9,13},{10,... | collective-permute-start | bytes 393224 | tf_op jit(solution)/shard_map/ppermute | solution.py:313
  27.8 33.3 %collective-permute-start.15 = (bf16[64,1024]{1,0:T(8,128)(2,1)}, bf16[64,1024]{1,0:T(8,128)(2,1)}, u32[]{:S(2)}, u32[]{:S(2)}) collective-permute-start(bf16[64,1024]{1,0:T(8,128)(2,1)} %slice.111.refs_0_), channel_id=1, source_target_pairs={{0,2},{1,3},{2,0},{3,1},{4,6},{5,7},{6,4},{7,5},{8,10},{9,11},{10,... | collective-permute-start | bytes 393224 | tf_op jit(solution)/shard_map/ppermute | solution.py:313
  43.0 12.7 %collective-permute-start.9 = (bf16[64,4096]{1,0:T(8,128)(2,1)}, bf16[64,4096]{1,0:T(8,128)(2,1)}, u32[]{:S(2)}, u32[]{:S(2)}) collective-permute-start(bf16[64,4096]{1,0:T(8,128)(2,1)} %slice.139), channel_id=1, source_target_pairs={{0,8},{8,0},{16,24},{24,16},{1,9},{9,1},{17,25},{25,17},{2,10},{10... | collective-permute-start | bytes 1572872 | tf_op jit(solution)/shard_map/ppermute | solution.py:313
  45.6 16.4 %collective-permute-start.10 = (bf16[64,4096]{1,0:T(8,128)(2,1)S(1)}, bf16[64,4096]{1,0:T(8,128)(2,1)S(1)}, u32[]{:S(2)}, u32[]{:S(2)}) collective-permute-start(bf16[64,4096]{1,0:T(8,128)(2,1)S(1)} %slice.140), channel_id=1, source_target_pairs={{0,16},{8,24},{16,0},{24,8},{1,17},{9,25},{17,1},{25,9},{2,18},{10... | collective-permute-start | bytes 1572872 | tf_op jit(solution)/shard_map/ppermute | solution.py:313
  49.6 11.5 %collective-permute-start.14 = (bf16[64,1024]{1,0:T(8,128)(2,1)}, bf16[64,1024]{1,0:T(8,128)(2,1)S(1)}, u32[]{:S(2)}, u32[]{:S(2)}) collective-permute-start(bf16[64,1024]{1,0:T(8,128)(2,1)} %slice.111.refs_0_), channel_id=1, source_target_pairs={{0,1},{1,0},{2,3},{3,2},{4,5},{5,4},{6,7},{7,6},{8,9},{9,8},{10,11... | collective-permute-start | bytes 393224 | tf_op jit(solution)/shard_map/ppermute | solution.py:313
  55.8 6.3 %collective-permute-start.20 = (bf16[64,1024]{1,0:T(8,128)(2,1)}, bf16[64,1024]{1,0:T(8,128)(2,1)S(1)}, u32[]{:S(2)}, u32[]{:S(2)}) collective-permute-start(bf16[64,1024]{1,0:T(8,128)(2,1)} %collective-permute-done.19.refs_6_), channel_id=1, source_target_pairs={{0,1},{1,0},{2,3},{3,2},{4,5},{5,4},{6,7},{7,6},{8,9},{9,8},{10,11... | collective-permute-start | bytes 393224 | tf_op jit(solution)/shard_map/ppermute | solution.py:313
  57.7 13.9 %collective-permute-start.5 = (bf16[64,3072]{1,0:T(8,128)(2,1)S(1)}, bf16[64,3072]{1,0:T(8,128)(2,1)S(1)}, u32[]{:S(2)}, u32[]{:S(2)}) collective-permute-start(bf16[64,3072]{1,0:T(8,128)(2,1)S(1)} %slice.105.refs_0_), channel_id=1, source_target_pairs={{0,6},{1,7},{2,4},{3,5},{4,2},{5,3},{6,0},{7,1},{8,14},{9,15},{10,... | collective-permute-start | bytes 1179656 | tf_op jit(solution)/shard_map/ppermute | solution.py:313
  61.1 34.3 %collective-permute-start.3 = (bf16[64,3072]{1,0:T(8,128)(2,1)S(1)}, bf16[64,3072]{1,0:T(8,128)(2,1)}, u32[]{:S(2)}, u32[]{:S(2)}) collective-permute-start(bf16[64,3072]{1,0:T(8,128)(2,1)S(1)} %slice.105.refs_0_), channel_id=1, source_target_pairs={{0,4},{1,5},{2,6},{3,7},{4,0},{5,1},{6,2},{7,3},{8,12},{9,13},{10,... | collective-permute-start | bytes 1179656 | tf_op jit(solution)/shard_map/ppermute | solution.py:313
  61.1 34.3 %copy-start.20 = (bf16[64,1024]{1,0:T(8,128)(2,1)}, bf16[64,1024]{1,0:T(8,128)(2,1)S(1)}, u32[]{:S(2)}) copy-start(bf16[64,1024]{1,0:T(8,128)(2,1)S(1)} %collective-permute-done.14.refs_1_) | copy-start | bytes 393220
  61.1 34.3 %collective-permute-start.1 = (bf16[64,3072]{1,0:T(8,128)(2,1)S(1)}, bf16[64,3072]{1,0:T(8,128)(2,1)}, u32[]{:S(2)}, u32[]{:S(2)}) collective-permute-start(bf16[64,3072]{1,0:T(8,128)(2,1)S(1)} %slice.105.refs_0_), channel_id=1, source_target_pairs={{0,2},{1,3},{2,0},{3,1},{4,6},{5,7},{6,4},{7,5},{8,10},{9,11},{10,... | collective-permute-start | bytes 1179656 | tf_op jit(solution)/shard_map/ppermute | solution.py:313
  62.1 33.9 %copy-start.21 = (bf16[64,1024]{1,0:T(8,128)(2,1)}, bf16[64,1024]{1,0:T(8,128)(2,1)S(1)}, u32[]{:S(2)}) copy-start(bf16[64,1024]{1,0:T(8,128)(2,1)S(1)} %collective-permute-done.20.refs_7_) | copy-start | bytes 393220
  62.1 1.6 collective-permute-start.18
  62.1 33.9 %collective-permute-start.16 = (bf16[64,1024]{1,0:T(8,128)(2,1)}, bf16[64,1024]{1,0:T(8,128)(2,1)}, u32[]{:S(2)}, u32[]{:S(2)}) collective-permute-start(bf16[64,1024]{1,0:T(8,128)(2,1)} %collective-permute-done.15.refs_2_), channel_id=1, source_target_pairs={{0,1},{1,0},{2,3},{3,2},{4,5},{5,4},{6,7},{7,6},{8,9},{9,8},{10,11... | collective-permute-start | bytes 393224 | tf_op jit(solution)/shard_map/ppermute | solution.py:313
  63.6 83.1 %collective-permute-start = (bf16[64,3072]{1,0:T(8,128)(2,1)S(1)}, bf16[64,3072]{1,0:T(8,128)(2,1)}, u32[]{:S(2)}, u32[]{:S(2)}) collective-permute-start(bf16[64,3072]{1,0:T(8,128)(2,1)S(1)} %slice.105.refs_0_), channel_id=1, source_target_pairs={{0,1},{1,0},{2,3},{3,2},{4,5},{5,4},{6,7},{7,6},{8,9},{9,8},{10,11... | collective-permute-start | bytes 1179656 | tf_op jit(solution)/shard_map/ppermute | solution.py:313
  71.6 75.1 %copy-start.7 = (bf16[64,3072]{1,0:T(8,128)(2,1)}, bf16[64,3072]{1,0:T(8,128)(2,1)S(1)}, u32[]{:S(2)}) copy-start(bf16[64,3072]{1,0:T(8,128)(2,1)S(1)} %collective-permute-done.5.refs_6_) | copy-start | bytes 1179652
  71.6 75.1 %collective-permute-start.6 = (bf16[64,3072]{1,0:T(8,128)(2,1)S(1)}, bf16[64,3072]{1,0:T(8,128)(2,1)}, u32[]{:S(2)}, u32[]{:S(2)}) collective-permute-start(bf16[64,3072]{1,0:T(8,128)(2,1)S(1)} %collective-permute-done.5.refs_6_), channel_id=1, source_target_pairs={{0,1},{1,0},{2,3},{3,2},{4,5},{5,4},{6,7},{7,6},{8,9},{9,8},{10,11... | collective-permute-start | bytes 1179656 | tf_op jit(solution)/shard_map/ppermute | solution.py:313
  95.4 51.3 %collective-permute-start.4 = (bf16[64,3072]{1,0:T(8,128)(2,1)}, bf16[64,3072]{1,0:T(8,128)(2,1)}, u32[]{:S(2)}, u32[]{:S(2)}) collective-permute-start(bf16[64,3072]{1,0:T(8,128)(2,1)} %collective-permute-done.3.refs_4_), channel_id=1, source_target_pairs={{0,1},{1,0},{2,3},{3,2},{4,5},{5,4},{6,7},{7,6},{8,9},{9,8},{10,11... | collective-permute-start | bytes 1179656 | tf_op jit(solution)/shard_map/ppermute | solution.py:313
  95.4 51.3 %collective-permute-start.2 = (bf16[64,3072]{1,0:T(8,128)(2,1)}, bf16[64,3072]{1,0:T(8,128)(2,1)}, u32[]{:S(2)}, u32[]{:S(2)}) collective-permute-start(bf16[64,3072]{1,0:T(8,128)(2,1)} %collective-permute-done.1.refs_2_), channel_id=1, source_target_pairs={{0,1},{1,0},{2,3},{3,2},{4,5},{5,4},{6,7},{7,6},{8,9},{9,8},{10,11... | collective-permute-start | bytes 1179656 | tf_op jit(solution)/shard_map/ppermute | solution.py:313
  272.9 64.9 %copy-start.10 = (bf16[128,2048]{1,0:T(8,128)(2,1)S(1)}, bf16[128,2048]{1,0:T(8,128)(2,1)}, u32[]{:S(2)}) copy-start(bf16[128,2048]{1,0:T(8,128)(2,1)} %get-tuple-element.35) | copy-start | bytes 1572868
  304.0 60.7 %copy-start.6 = (f32[4,64,2048]{2,1,0:T(8,128)S(1)}, f32[4,64,2048]{2,1,0:T(8,128)}, u32[]{:S(2)}) copy-start(f32[4,64,2048]{2,1,0:T(8,128)} %get-tuple-element.47) | copy-start | bytes 6291460
  306.0 5.0 %collective-permute-start.40 = (f32[3,4096]{1,0:T(4,128)S(1)}, f32[3,4096]{1,0:T(4,128)S(1)}, u32[]{:S(2)}, u32[]{:S(2)}) collective-permute-start(f32[3,4096]{1,0:T(4,128)S(1)} %fusion.20), channel_id=1, source_target_pairs={{0,16},{8,24},{16,0},{24,8},{1,17},{9,25},{17,1},{25,9},{2,18},{10... | collective-permute-start | bytes 147464 | tf_op jit(solution)/shard_map/ppermute | solution.py:313
  307.4 5.7 %collective-permute-start.41 = (f32[3,4096]{1,0:T(4,128)S(1)}, f32[3,4096]{1,0:T(4,128)S(1)}, u32[]{:S(2)}, u32[]{:S(2)}) collective-permute-start(f32[3,4096]{1,0:T(4,128)S(1)} %fusion.20), channel_id=1, source_target_pairs={{0,24},{8,16},{16,8},{24,0},{1,25},{9,17},{17,9},{25,1},{2,26},{10... | collective-permute-start | bytes 147464 | tf_op jit(solution)/shard_map/ppermute | solution.py:313
  309.0 5.4 %collective-permute-start.39 = (f32[3,4096]{1,0:T(4,128)S(1)}, f32[3,4096]{1,0:T(4,128)S(1)}, u32[]{:S(2)}, u32[]{:S(2)}) collective-permute-start(f32[3,4096]{1,0:T(4,128)S(1)} %fusion.20), channel_id=1, source_target_pairs={{0,8},{8,0},{16,24},{24,16},{1,9},{9,1},{17,25},{25,17},{2,10},{10... | collective-permute-start | bytes 147464 | tf_op jit(solution)/shard_map/ppermute | solution.py:313
  309.6 28.6 %collective-permute-start.27 = (bf16[4,64,1024]{2,1,0:T(8,128)(2,1)}, bf16[4,64,1024]{2,1,0:T(8,128)(2,1)S(1)}, u32[]{:S(2)}, u32[]{:S(2)}) collective-permute-start(bf16[4,64,1024]{2,1,0:T(8,128)(2,1)} %get-tuple-element.46), channel_id=1, source_target_pairs={{0,1},{1,0},{2,3},{3,2},{4,5},{5,4},{6,7},{7,6},{8,9},{9,8},{10,11... | collective-permute-start | bytes 1572872 | tf_op jit(solution)/shard_map/ppermute | solution.py:313
  309.6 15.3 %collective-permute-start.21 = (bf16[128,2048]{1,0:T(8,128)(2,1)}, bf16[128,2048]{1,0:T(8,128)(2,1)S(1)}, u32[]{:S(2)}, u32[]{:S(2)}) collective-permute-start(bf16[128,2048]{1,0:T(8,128)(2,1)} %get-tuple-element.36), channel_id=1, source_target_pairs={{0,8},{8,0},{16,24},{24,16},{1,9},{9,1},{17,25},{25,17},{2,10},{10... | collective-permute-start | bytes 1572872 | tf_op jit(solution)/shard_map/ppermute | solution.py:313
  311.0 25.5 %collective-permute-start.22 = (bf16[128,2048]{1,0:T(8,128)(2,1)}, bf16[128,2048]{1,0:T(8,128)(2,1)S(1)}, u32[]{:S(2)}, u32[]{:S(2)}) collective-permute-start(bf16[128,2048]{1,0:T(8,128)(2,1)} %get-tuple-element.37), channel_id=1, source_target_pairs={{0,16},{8,24},{16,0},{24,8},{1,17},{9,25},{17,1},{25,9},{2,18},{10... | collective-permute-start | bytes 1572872 | tf_op jit(solution)/shard_map/ppermute | solution.py:313
  313.1 24.6 %collective-permute-start.23 = (bf16[128,2048]{1,0:T(8,128)(2,1)}, bf16[128,2048]{1,0:T(8,128)(2,1)S(1)}, u32[]{:S(2)}, u32[]{:S(2)}) collective-permute-start(bf16[128,2048]{1,0:T(8,128)(2,1)} %get-tuple-element.38), channel_id=1, source_target_pairs={{0,24},{8,16},{16,8},{24,0},{1,25},{9,17},{17,9},{25,1},{2,26},{10... | collective-permute-start | bytes 1572872 | tf_op jit(solution)/shard_map/ppermute | solution.py:313
  314.4 33.0 %collective-permute-start.24 = (bf16[128,2048]{1,0:T(8,128)(2,1)}, bf16[128,2048]{1,0:T(8,128)(2,1)S(1)}, u32[]{:S(2)}, u32[]{:S(2)}) collective-permute-start(bf16[128,2048]{1,0:T(8,128)(2,1)} %get-tuple-element.42), channel_id=1, source_target_pairs={{0,8},{8,0},{16,24},{24,16},{1,9},{9,1},{17,25},{25,17},{2,10},{10... | collective-permute-start | bytes 1572872 | tf_op jit(solution)/shard_map/ppermute | solution.py:313
  324.9 33.0 %collective-permute-start.25 = (bf16[128,2048]{1,0:T(8,128)(2,1)}, bf16[128,2048]{1,0:T(8,128)(2,1)S(1)}, u32[]{:S(2)}, u32[]{:S(2)}) collective-permute-start(bf16[128,2048]{1,0:T(8,128)(2,1)} %get-tuple-element.43), channel_id=1, source_target_pairs={{0,16},{8,24},{16,0},{24,8},{1,17},{9,25},{17,1},{25,9},{2,18},{10... | collective-permute-start | bytes 1572872 | tf_op jit(solution)/shard_map/ppermute | solution.py:313
  336.5 22.5 %collective-permute-start.26 = (bf16[128,2048]{1,0:T(8,128)(2,1)}, bf16[128,2048]{1,0:T(8,128)(2,1)S(1)}, u32[]{:S(2)}, u32[]{:S(2)}) collective-permute-start(bf16[128,2048]{1,0:T(8,128)(2,1)} %get-tuple-element.44), channel_id=1, source_target_pairs={{0,24},{8,16},{16,8},{24,0},{1,25},{9,17},{17,9},{25,1},{2,26},{10... | collective-permute-start | bytes 1572872 | tf_op jit(solution)/shard_map/ppermute | solution.py:313
  337.8 2.1 collective-permute-start.35
  338.1 25.2 %collective-permute-start.31 = (bf16[4,64,2048]{2,1,0:T(8,128)(2,1)}, bf16[4,64,2048]{2,1,0:T(8,128)(2,1)S(1)}, u32[]{:S(2)}, u32[]{:S(2)}) collective-permute-start(bf16[4,64,2048]{2,1,0:T(8,128)(2,1)} %get-tuple-element.48), channel_id=1, source_target_pairs={{0,1},{1,0},{2,3},{3,2},{4,5},{5,4},{6,7},{7,6},{8,9},{9,8},{10,11... | collective-permute-start | bytes 3145736 | tf_op jit(solution)/shard_map/ppermute | solution.py:313
  339.9 25.0 %collective-permute-start.28 = (bf16[64,1024]{1,0:T(8,128)(2,1)S(1)}, bf16[64,1024]{1,0:T(8,128)(2,1)S(1)}, u32[]{:S(2)}, u32[]{:S(2)}) collective-permute-start(bf16[64,1024]{1,0:T(8,128)(2,1)S(1)} %get-tuple-element.65), channel_id=1, source_target_pairs={{0,2},{1,3},{2,0},{3,1},{4,6},{5,7},{6,4},{7,5},{8,10},{9,11},{10,... | collective-permute-start | bytes 393224 | tf_op jit(solution)/shard_map/ppermute | solution.py:313
  347.4 17.8 %collective-permute-start.30 = (bf16[64,1024]{1,0:T(8,128)(2,1)S(1)}, bf16[64,1024]{1,0:T(8,128)(2,1)S(1)}, u32[]{:S(2)}, u32[]{:S(2)}) collective-permute-start(bf16[64,1024]{1,0:T(8,128)(2,1)S(1)} %get-tuple-element.66), channel_id=1, source_target_pairs={{0,6},{1,7},{2,4},{3,5},{4,2},{5,3},{6,0},{7,1},{8,14},{9,15},{10,... | collective-permute-start | bytes 393224 | tf_op jit(solution)/shard_map/ppermute | solution.py:313
  357.9 10.1 %collective-permute-start.29 = (bf16[64,1024]{1,0:T(8,128)(2,1)S(1)}, bf16[64,1024]{1,0:T(8,128)(2,1)S(1)}, u32[]{:S(2)}, u32[]{:S(2)}) collective-permute-start(bf16[64,1024]{1,0:T(8,128)(2,1)S(1)} %get-tuple-element.67), channel_id=1, source_target_pairs={{0,4},{1,5},{2,6},{3,7},{4,0},{5,1},{6,2},{7,3},{8,12},{9,13},{10,... | collective-permute-start | bytes 393224 | tf_op jit(solution)/shard_map/ppermute | solution.py:313
  359.0 10.4 %collective-permute-start.36 = (bf16[64,1024]{1,0:T(8,128)(2,1)S(1)}, bf16[64,1024]{1,0:T(8,128)(2,1)S(1)}, u32[]{:S(2)}, u32[]{:S(2)}) collective-permute-start(bf16[64,1024]{1,0:T(8,128)(2,1)S(1)} %get-tuple-element.68), channel_id=1, source_target_pairs={{0,2},{1,3},{2,0},{3,1},{4,6},{5,7},{6,4},{7,5},{8,10},{9,11},{10,... | collective-permute-start | bytes 393224 | tf_op jit(solution)/shard_map/ppermute | solution.py:313
  363.4 8.2 %collective-permute-start.38 = (bf16[64,1024]{1,0:T(8,128)(2,1)S(1)}, bf16[64,1024]{1,0:T(8,128)(2,1)S(1)}, u32[]{:S(2)}, u32[]{:S(2)}) collective-permute-start(bf16[64,1024]{1,0:T(8,128)(2,1)S(1)} %get-tuple-element.69), channel_id=1, source_target_pairs={{0,6},{1,7},{2,4},{3,5},{4,2},{5,3},{6,0},{7,1},{8,14},{9,15},{10,... | collective-permute-start | bytes 393224 | tf_op jit(solution)/shard_map/ppermute | solution.py:313
  364.9 14.9 %collective-permute-start.37 = (bf16[64,1024]{1,0:T(8,128)(2,1)S(1)}, bf16[64,1024]{1,0:T(8,128)(2,1)S(1)}, u32[]{:S(2)}, u32[]{:S(2)}) collective-permute-start(bf16[64,1024]{1,0:T(8,128)(2,1)S(1)} %get-tuple-element.70), channel_id=1, source_target_pairs={{0,4},{1,5},{2,6},{3,7},{4,0},{5,1},{6,2},{7,3},{8,12},{9,13},{10,... | collective-permute-start | bytes 393224 | tf_op jit(solution)/shard_map/ppermute | solution.py:313
  365.2 15.6 %collective-permute-start.32 = (bf16[64,2048]{1,0:T(8,128)(2,1)S(1)}, bf16[64,2048]{1,0:T(8,128)(2,1)S(1)}, u32[]{:S(2)}, u32[]{:S(2)}) collective-permute-start(bf16[64,2048]{1,0:T(8,128)(2,1)S(1)} %get-tuple-element.62), channel_id=1, source_target_pairs={{0,2},{1,3},{2,0},{3,1},{4,6},{5,7},{6,4},{7,5},{8,10},{9,11},{10,... | collective-permute-start | bytes 786440 | tf_op jit(solution)/shard_map/ppermute | solution.py:313
  368.0 17.7 %collective-permute-start.34 = (bf16[64,2048]{1,0:T(8,128)(2,1)S(1)}, bf16[64,2048]{1,0:T(8,128)(2,1)S(1)}, u32[]{:S(2)}, u32[]{:S(2)}) collective-permute-start(bf16[64,2048]{1,0:T(8,128)(2,1)S(1)} %get-tuple-element.63), channel_id=1, source_target_pairs={{0,6},{1,7},{2,4},{3,5},{4,2},{5,3},{6,0},{7,1},{8,14},{9,15},{10,... | collective-permute-start | bytes 786440 | tf_op jit(solution)/shard_map/ppermute | solution.py:313
  369.4 29.4 %collective-permute-start.33 = (bf16[64,2048]{1,0:T(8,128)(2,1)S(1)}, bf16[64,2048]{1,0:T(8,128)(2,1)S(1)}, u32[]{:S(2)}, u32[]{:S(2)}) collective-permute-start(bf16[64,2048]{1,0:T(8,128)(2,1)S(1)} %get-tuple-element.64), channel_id=1, source_target_pairs={{0,4},{1,5},{2,6},{3,7},{4,0},{5,1},{6,2},{7,3},{8,12},{9,13},{10,... | collective-permute-start | bytes 786440 | tf_op jit(solution)/shard_map/ppermute | solution.py:313
  (17 other events, 359.4 us)
